TPU v7x, 512 devices: a whole 4x4x16 slice. The times are simulated.
512 devices in a mesh: req: 32 (over z, core), mlp: 16 (over y, x).
Axes of the slice: x: 4, y: 4, z: 16, core: 2. Of those that a mesh axis runs over, the one named last changes fastest.
Arguments:
- hidden_input: bfloat16 [12288, 4096], P('req', 'mlp'), may hold values from -6 to 6
- input_norm_gain: bfloat16 [4096], replicated, may hold values from 0.099609375 to 1.8984375
- query_norm_gain: bfloat16 [128], replicated, may hold values from 0.099609375 to 1.8984375
- key_norm_gain: bfloat16 [128], replicated, may hold values from 0.099609375 to 1.8984375
- query_weight: bfloat16 [4096, 4096], P('req', 'mlp'), may hold values from -0.09375 to 0.09375
- key_value_weight: bfloat16 [4096, 2, 1024], P('req'), may hold values from -0.09375 to 0.09375
- output_weight: bfloat16 [4096, 16, 256], P('mlp', None, 'req'), may hold values from -0.09375 to 0.09375
- adapter_down_qkv: bfloat16 [64, 48, 4096], P('req', None, 'mlp'), may hold values from -0.09375 to 0.09375
- adapter_down_output: bfloat16 [64, 16, 4096], P('req', None, 'mlp'), may hold values from -0.09375 to 0.09375
- adapter_up_query: bfloat16 [64, 16, 4096], P('req', None, 'mlp'), may hold values from -1.5 to 1.5
- adapter_up_key_value: bfloat16 [64, 16, 2, 1024], P('req'), may hold values from -1.5 to 1.5
- adapter_up_output: bfloat16 [64, 16, 4096], P('req', None, 'mlp'), may hold values from -1.5 to 1.5
- pool: bfloat16 [16384, 2, 1024], P('req'), may hold values from -6 to 6
- lengths: int32 [32, 4], P('req'), may hold values from 1 to 192, 384 in all within a row
- cached_prefix_pages: int32 [32, 4], P('req'), may hold values from 0 to 8
- prefix_page_table: int32 [32, 4, 8], P('req'), may hold values from 0 to 7, each once within a row
- adapter_of_request: int32 [32, 4, 1], P('req'), may hold values from 0 to 63
- adapter_storage: int32 [64], replicated, may hold values from 0 to 63, each once
Outputs:
- attention_update: bfloat16 [12288, 4096], P('req', 'mlp')
- new_cache: bfloat16 [12288, 2, 1024], P('req', None, 'mlp')
Inputs may be any that keep to these rules, and one draw needn't show every extreme that they name: The lengths of one index of req sum to 384, and the longest of them is 192. `prefix_page_table`: each row lists every page of its pool once. `adapter_of_request`: every adapter is used by some request. `adapter_storage`: each slot holds one adapter.
All inputs are finite; a program needn't handle non-finite values.
Results may differ from a plain program's by a relative error of at most 0.035.
Values may be sent and summed in bfloat16 or wider, within the bound.
A program may use at most 64 MiB of HBM per device.

v0:
```python
import math
import jax
import jax.numpy as jnp
from jax import lax
from jax.sharding import PartitionSpec as P

QUERY_HEADS = 32
KEY_VALUE_HEADS = 8
HEAD_SIZE = 128
ADAPTER_RANK = 16
PAGE = 64
epsilon = 1e-06
rope_base = 1000000.0


def root_mean_scale(values, gain_vec):
    mean_sq = jnp.mean(values * values, axis=-1, keepdims=True)
    return values * lax.rsqrt(mean_sq + epsilon) * gain_vec.astype(jnp.float32)


def rotary_embed(values, token_positions):
    half_width = values.shape[-1] // 2
    inverse_freq = jnp.exp(
        jnp.arange(half_width, dtype=jnp.float32) * (-2.0 / values.shape[-1]) * math.log(rope_base)
    )
    angles = token_positions.astype(jnp.float32)[:, None] * inverse_freq[None, :]
    cosine = jnp.cos(angles)[:, None, :]
    sine_part = jnp.sin(angles)[:, None, :]
    front = values[..., :half_width]
    back = values[..., half_width:]
    return jnp.concatenate(
        [front * cosine - back * sine_part, back * cosine + front * sine_part], axis=-1
    )


def row_tables(lengths_row, prefix_row, page_rows, row_count):
    ends_at = jnp.cumsum(lengths_row)
    starts_at = ends_at - lengths_row
    row_ids = jnp.arange(row_count, dtype=jnp.int32)
    owners = jnp.sum((row_ids[:, None] >= ends_at[None, :]).astype(jnp.int32), axis=1)
    group_members = owners[:, None] == jnp.arange(lengths_row.shape[0], dtype=jnp.int32)[None, :]
    offsets = PAGE * prefix_row[None, :] + row_ids[:, None] - starts_at[None, :]
    token_positions = jnp.sum(jnp.where(group_members, offsets, 0), axis=1)
    page_ids = jnp.arange(page_rows.shape[1], dtype=jnp.int32)
    listed = (page_rows[:, :, None] == page_ids[None, None, :]) & (
        page_ids[None, :, None] < prefix_row[:, None, None]
    )
    page_used = jnp.sum(listed.astype(jnp.float32), axis=1)
    return (owners, group_members, token_positions, page_used)


def apply_adapter(lowrank_inner, group_members, chosen_up):
    masked = lowrank_inner[:, None, :] * group_members.astype(lowrank_inner.dtype)[:, :, None]
    return jnp.einsum("gjr,jrc->gc", masked, chosen_up, preferred_element_type=jnp.float32)


def select_rows(terms, group_members):
    return jnp.sum(terms * group_members.astype(jnp.float32)[:, :, None], axis=1)


def shards(
    hidden_input,
    input_norm_gain,
    query_norm_gain,
    key_norm_gain,
    query_weight,
    key_value_weight,
    output_weight,
    adapter_down_qkv,
    adapter_down_output,
    adapter_up_query,
    adapter_up_key_value,
    adapter_up_output,
    pool,
    lengths,
    cached_prefix_pages,
    prefix_page_table,
    adapter_of_request,
    adapter_storage,
):
    feature_group_count = lax.axis_size("mlp")
    feature_group_index = lax.axis_index("mlp")
    whole = lax.all_gather(hidden_input, "mlp", axis=1, tiled=True)
    row_count, full_width = whole.shape
    normalized_input = root_mean_scale(whole.astype(jnp.float32), input_norm_gain).astype(
        jnp.bfloat16
    )
    owners, group_members, token_positions, page_used = row_tables(
        lengths[0], cached_prefix_pages[0], prefix_page_table[0], row_count
    )
    q_width = query_weight.shape[1]
    query_head_rows = q_width // HEAD_SIZE
    key_value_local = max(1, KEY_VALUE_HEADS // feature_group_count)
    key_value_width = key_value_local * HEAD_SIZE
    key_value_begin = (
        feature_group_index * query_head_rows // (QUERY_HEADS // KEY_VALUE_HEADS) * HEAD_SIZE
    )
    own_wkv = lax.dynamic_slice_in_dim(key_value_weight, key_value_begin, key_value_width, 2)
    request_key_value_up = lax.dynamic_slice_in_dim(
        adapter_up_key_value, key_value_begin, key_value_width, 3
    )
    gathered = (
        lax.all_gather(adapter_down_qkv, "req", axis=0, tiled=True),
        lax.all_gather(adapter_down_output, "req", axis=0, tiled=True),
        lax.all_gather(adapter_up_query, "req", axis=0, tiled=True),
        lax.all_gather(request_key_value_up, "req", axis=0, tiled=True),
        lax.all_gather(adapter_up_output, "req", axis=0, tiled=True),
    )
    slot_indices = jnp.take(adapter_storage, adapter_of_request[0, :, 0], axis=0)
    chosen_down = jnp.take(gathered[0], slot_indices, axis=0)
    output_down = jnp.take(gathered[1], slot_indices, axis=0)
    query_up_part = jnp.take(gathered[2], slot_indices, axis=0)
    key_value_up = jnp.take(gathered[3], slot_indices, axis=0)
    output_up = jnp.take(gathered[4], slot_indices, axis=0)
    feature_cols = full_width // feature_group_count
    own_normed = lax.dynamic_slice_in_dim(
        normalized_input, feature_group_index * feature_cols, feature_cols, 1
    )
    low_terms = jnp.einsum(
        "gd,jkd->gjk", own_normed, chosen_down, preferred_element_type=jnp.float32
    )
    lowrank_inner = lax.psum(select_rows(low_terms, group_members).astype(jnp.bfloat16), "mlp")
    q_part = lax.all_gather(query_weight, "req", axis=0, tiled=True)
    kv_part = lax.all_gather(own_wkv, "req", axis=0, tiled=True)
    query_width_total = jnp.dot(normalized_input, q_part, preferred_element_type=jnp.float32)
    kv_total = jnp.dot(
        normalized_input,
        kv_part.reshape(kv_part.shape[0], 2 * key_value_width),
        preferred_element_type=jnp.float32,
    )
    query_width_total, kv_total = (query_width_total, kv_total)
    query_plain = (
        query_width_total
        + apply_adapter(lowrank_inner[:, 0:ADAPTER_RANK], group_members, query_up_part)
    ).astype(jnp.bfloat16)
    key_lowrank_part = apply_adapter(
        lowrank_inner[:, ADAPTER_RANK : 2 * ADAPTER_RANK], group_members, key_value_up[:, :, 0]
    )
    value_lowrank_part = apply_adapter(
        lowrank_inner[:, 2 * ADAPTER_RANK : 3 * ADAPTER_RANK], group_members, key_value_up[:, :, 1]
    )
    key_value_plain = (
        kv_total.reshape(row_count, 2, key_value_width)
        + jnp.stack([key_lowrank_part, value_lowrank_part], axis=1)
    ).astype(jnp.bfloat16)
    cached = lax.dynamic_slice_in_dim(pool, key_value_begin, key_value_width, 2)
    pool_token_rows = cached.shape[0]
    query_rotated = rotary_embed(
        root_mean_scale(
            query_plain.astype(jnp.float32).reshape(row_count, query_head_rows, HEAD_SIZE),
            query_norm_gain,
        ),
        token_positions,
    ).astype(jnp.bfloat16)
    key_rotated = rotary_embed(
        root_mean_scale(
            key_value_plain[:, 0]
            .astype(jnp.float32)
            .reshape(row_count, key_value_local, HEAD_SIZE),
            key_norm_gain,
        ),
        token_positions,
    ).astype(jnp.bfloat16)
    cache_columns = KEY_VALUE_HEADS * HEAD_SIZE // feature_group_count
    own_offset = feature_group_index * cache_columns - key_value_begin
    local_cache = jnp.stack(
        [key_rotated.reshape(row_count, key_value_width), key_value_plain[:, 1]], axis=1
    )
    new_cache = lax.dynamic_slice_in_dim(local_cache, own_offset, cache_columns, 2)
    key_matrix = jnp.concatenate(
        [cached[:, 0].reshape(pool_token_rows, key_value_local, HEAD_SIZE), key_rotated], axis=0
    )
    value_matrix = jnp.concatenate(
        [
            cached[:, 1].reshape(pool_token_rows, key_value_local, HEAD_SIZE),
            key_value_plain[:, 1].reshape(row_count, key_value_local, HEAD_SIZE),
        ],
        axis=0,
    )
    pool_ok = jnp.dot(group_members.astype(jnp.float32), page_used, precision=lax.Precision.HIGHEST)
    pool_ok = jnp.repeat(pool_ok, PAGE, axis=1) > 0.5
    row_ids = jnp.arange(row_count, dtype=jnp.int32)
    causal = (owners[:, None] == owners[None, :]) & (row_ids[None, :] <= row_ids[:, None])
    allowed = jnp.concatenate([pool_ok, causal], axis=1)
    query_rows = query_rotated.reshape(
        row_count, key_value_local, query_head_rows // key_value_local, HEAD_SIZE
    )
    scores = jnp.einsum(
        "gkhd,skd->khgs", query_rows, key_matrix, preferred_element_type=jnp.float32
    ) / math.sqrt(HEAD_SIZE)
    exp_scores = jnp.where(allowed[None, None], jnp.exp(scores), 0.0)
    softmax = (exp_scores / jnp.sum(exp_scores, axis=-1, keepdims=True)).astype(jnp.bfloat16)
    attended = jnp.einsum(
        "khgs,skd->gkhd", softmax, value_matrix, preferred_element_type=jnp.float32
    )
    attended = attended.astype(jnp.bfloat16).reshape(row_count, q_width)
    out_terms = jnp.einsum("gc,jrc->gjr", attended, output_down, preferred_element_type=jnp.float32)
    lowrank_result = lax.psum(select_rows(out_terms, group_members), "mlp").astype(jnp.bfloat16)
    partial_value = jnp.einsum(
        "gc,cnk->gnk",
        attended,
        lax.all_gather(output_weight, "req", axis=2, tiled=True),
        preferred_element_type=jnp.float32,
    )
    summed_output = lax.psum_scatter(
        partial_value.reshape(row_count, full_width).astype(jnp.bfloat16),
        "mlp",
        scatter_dimension=1,
        tiled=True,
    ).astype(jnp.float32)
    attention_update = (
        summed_output + apply_adapter(lowrank_result, group_members, output_up)
    ).astype(jnp.bfloat16)
    return (attention_update, new_cache)


def solution(mesh):
    return jax.shard_map(
        shards,
        mesh=mesh,
        in_specs=(
            P("req", "mlp"),
            P(),
            P(),
            P(),
            P("req", "mlp"),
            P("req", None, None),
            P("mlp", None, "req"),
            P("req", None, "mlp"),
            P("req", None, "mlp"),
            P("req", None, "mlp"),
            P("req", None, None, None),
            P("req", None, "mlp"),
            P("req", None, None),
            P("req", None),
            P("req", None),
            P("req", None, None),
            P("req", None, None),
            P(),
        ),
        out_specs=(P("req", "mlp"), P("req", None, "mlp")),
        check_vma=False,
    )
```

profile of v0, /device:TPU:32, one launch (start us, length us, event | category | flops | bytes accessed | tf_op | source)
XLA Modules:
  0.0 518.9 jit_solution(2938642543624137017)
XLA Ops:
  11.6 1.3 gather_fusion
  14.2 0.8 reduce-window.4
  16.5 0.7 constant_dynamic-slice_fusion.1
  17.3 36.1 %all_gather.30 = bf16[64,16,2,128]{3,1,2,0:T(8,128)(2,1)S(1)} all-gather(bf16[2,16,2,128]{3,1,2,0:T(8,128)(2,1)S(1)} %copy.66), channel_id=1, replica_groups=mesh['req'=32,'mlp'=16] {'req'}, dimensions={0}, use_global_device_ids=true | all-gather | bytes 540672 | tf_op jit(solution)/shard_map/all_gather | solution.py:106
  53.3 0.7 convert_element_type.100
  54.0 1.2 convert_element_type.109
  56.0 1.6 constant_dynamic-slice_fusion
  57.6 30.2 %all_gather.32 = bf16[64,16,256]{2,1,0:T(8,128)(2,1)S(1)} all-gather(bf16[2,16,256]{2,1,0:T(8,128)(2,1)S(1)} %copy-done.6), channel_id=1, replica_groups=mesh['req'=32,'mlp'=16] {'req'}, dimensions={0}, use_global_device_ids=true | all-gather | bytes 540672 | tf_op jit(solution)/shard_map/all_gather | solution.py:105
  90.7 1.2 gather_fusion.3
  91.8 0.8 multiply_cosine_fusion
  92.8 2.6 gather_fusion.1
  95.4 61.2 %all-gather.8.cloned.1.call-done = bf16[4096,2,128]{2,1,0:T(2,128)(2,1)} async-done(((bf16[128,2,128]{2,1,0:T(2,128)(2,1)}), bf16[4096,2,128]{2,1,0:T(2,128)(2,1)}) %all-gather.8.cloned.1.call-update) | async-done | bytes 2097168 | tf_op jit(solution)/shard_map/all_gather | solution.py:124
  156.6 4.7 copy.61
  161.3 63.1 %all-gather.6.cloned.1.call-done = bf16[384,4096]{1,0:T(8,128)(2,1)} async-done(((bf16[384,256]{1,0:T(8,128)(2,1)}), bf16[384,4096]{1,0:T(8,128)(2,1)}) %all-gather.6.cloned.1.call-update) | async-done | bytes 3145744 | tf_op jit(solution)/shard_map/all_gather | solution.py:83
  224.4 2.7 fusion
  227.3 1.1 fusion.2
  228.4 1.6 copy-done.2
  230.0 0.9 fusion.26
  230.9 72.8 %psum.14 = bf16[384,48]{0,1:T(8,128)(2,1)S(1)} all-reduce(bf16[384,48]{0,1:T(8,128)(2,1)} %fusion.26), channel_id=1, replica_groups=mesh['req'=32,'mlp'=16] {'mlp'}, use_global_device_ids=true, to_apply=%region_4.5 | all-reduce | flops 18432 | bytes 73728 | tf_op jit(solution)/shard_map/psum | solution.py:122
  303.7 0.9 convolution_bitcast_fusion.2
  304.7 0.9 convolution_bitcast_fusion.3
  305.6 3.2 fusion.17
  309.6 3.8 fusion.92
  314.5 0.9 fusion.5
  315.5 0.9 fusion.23
  316.4 53.5 %all-gather.14.cloned.1.call-done = bf16[256,16,256]{0,2,1:T(8,128)(2,1)} async-done(((bf16[256,16,8]{0,2,1:T(8,128)(2,1)}), bf16[256,16,256]{0,2,1:T(8,128)(2,1)}) %all-gather.14.cloned.1.call-update) | async-done | bytes 2097168 | tf_op jit(solution)/shard_map/all_gather | solution.py:202
  369.9 4.3 convolution_convert_fusion
  374.9 28.9 %all_gather.34 = bf16[64,16,256]{2,1,0:T(8,128)(2,1)S(1)} all-gather(bf16[2,16,256]{2,1,0:T(8,128)(2,1)S(1)} %copy-done.7), channel_id=1, replica_groups=mesh['req'=32,'mlp'=16] {'req'}, dimensions={0}, use_global_device_ids=true | all-gather | bytes 540672 | tf_op jit(solution)/shard_map/all_gather | solution.py:104
  404.3 30.1 %all_gather.35 = bf16[64,16,256]{2,1,0:T(8,128)(2,1)S(1)} all-gather(bf16[2,16,256]{2,1,0:T(8,128)(2,1)S(1)} %copy-done.8), channel_id=1, replica_groups=mesh['req'=32,'mlp'=16] {'req'}, dimensions={0}, use_global_device_ids=true | all-gather | bytes 540672 | tf_op jit(solution)/shard_map/all_gather | solution.py:107
  435.2 74.3 %psum.15 = bf16[384,16]{0,1:T(8,128)(2,1)S(1)} all-reduce(f32[384,16]{0,1:T(8,128)S(1)} %fusion.27), channel_id=1, replica_groups=mesh['req'=32,'mlp'=16] {'mlp'}, use_global_device_ids=true, to_apply=%region_12.14 | all-reduce | flops 6144 | bytes 36864 | tf_op jit(solution)/shard_map/psum | solution.py:198
  509.5 0.7 fusion.50
  510.2 1.9 fusion.16
  (94 shorter events, 14.7 us)
Async XLA Ops:
  7.2 1.1 copy-start
  7.2 81.2 %copy-start.17 = (s32[1,4]{1,0:T(1,128)S(1)}, s32[1,4]{1,0:T(1,128)}, u32[]{:S(2)}) copy-start(s32[1,4]{1,0:T(1,128)} %param.34) | copy-start | bytes 52
  7.2 50.4 %copy-start.6 = (bf16[2,16,256]{2,1,0:T(8,128)(2,1)S(1)}, bf16[2,16,256]{2,1,0:T(8,128)(2,1)}, u32[]{:S(2)}) copy-start(bf16[2,16,256]{2,1,0:T(8,128)(2,1)} %param.29) | copy-start | bytes 49156
  7.2 80.6 %copy-start.16 = (bf16[128]{0:T(256)(128)(2,1)S(1)}, bf16[128]{0:T(256)(128)(2,1)}, u32[]{:S(2)}) copy-start(bf16[128]{0:T(256)(128)(2,1)} %param.22) | copy-start | bytes 772
  7.2 81.2 %copy-start.13 = (s32[1,4,8]{2,1,0:T(4,128)S(1)}, s32[1,4,8]{2,1,0:T(4,128)}, u32[]{:S(2)}) copy-start(s32[1,4,8]{2,1,0:T(4,128)} %param.35) | copy-start | bytes 388
  7.2 85.5 %all-gather.10.cloned.1.call-start = ((), (), s32[]{:S(2)}) async-start(), calls=%async_computation.3 | async-start | bytes 1622016 | tf_op jit(solution)/shard_map/all_gather | solution.py:103
  8.0 148.6 %all-gather.8.cloned.1.call-start = ((), (), s32[]{:S(2)}) async-start(), calls=%async_computation.2 | async-start | bytes 2162688 | tf_op jit(solution)/shard_map/all_gather | solution.py:124
  8.9 215.5 %all-gather.6.cloned.1.call-start = ((), (), s32[]{:S(2)}) async-start(), calls=%async_computation.1 | async-start | bytes 3342336 | tf_op jit(solution)/shard_map/all_gather | solution.py:83
  9.7 299.9 %all-gather.12.cloned.1.call-start = ((), (), s32[]{:S(2)}) async-start(), calls=%async_computation.4 | async-start | bytes 2162688 | tf_op jit(solution)/shard_map/all_gather | solution.py:123
  10.3 359.6 %all-gather.14.cloned.1.call-start = ((), (), s32[]{:S(2)}) async-start(), calls=%async_computation.5 | async-start | bytes 2162688 | tf_op jit(solution)/shard_map/all_gather | solution.py:202
  10.8 499.4 %reduce-scatter.2.cloned.1.call-start = ((), (), s32[]{:S(2)}) async-start(), calls=%async_computation.6 | async-start | bytes 3342336 | tf_op jit(solution)/shard_map/reduce_scatter | solution.py:205
  14.2 147.1 %copy-start.11 = (f32[64]{0:T(128)}, f32[64]{0:T(128)S(1)}, u32[]{:S(2)}) copy-start(f32[64]{0:T(128)S(1)} %multiply_exponential_fusion) | copy-start | bytes 772
  224.4 2.8 copy-start.1
  227.3 2.8 copy-start.5
  227.3 2.8 copy-start.9
  228.4 1.7 copy-start.2
  305.6 3.3 copy-start.14
  305.6 3.4 copy-start.12
  309.6 3.9 copy-start.4
  309.6 4.5 copy-start.15
  314.3 1.2 copy-start.3
  374.1 0.7 copy-start.7
  374.1 30.2 %copy-start.8 = (bf16[2,16,256]{2,1,0:T(8,128)(2,1)S(1)}, bf16[2,16,256]{2,1,0:T(8,128)(2,1)}, u32[]{:S(2)}) copy-start(bf16[2,16,256]{2,1,0:T(8,128)(2,1)} %param.31) | copy-start | bytes 49156
  374.1 60.9 %copy-start.10 = (f32[384,4]{0,1:T(4,128)S(1)}, f32[384,4]{0,1:T(4,128)}, u32[]{:S(2)}) copy-start(f32[384,4]{0,1:T(4,128)} %get-tuple-element.17) | copy-start | bytes 18436
Sparse Core Ops, SparseCore 0:
  10.2 75.3 all-gather.9
  87.7 68.8 all-gather.7
  159.6 64.8 all-gather.5
  226.4 71.1 all-gather.11
  299.5 70.3 all-gather.13
  374.3 87.2 reduce-scatter.1
where the time goes:
time: 520 us; the launch traced here: 519 us
  blocking collectives  272 us (52%)
  waiting for transfers between devices  180 us (35%)
  matrix products  18.5 us (4%)
  local copies, waits for them, and re-layouts  18.3 us (4%)
  other arithmetic  14.7 us (3%)
  between operations  14.6 us (3%)
    psum x1, blocking collectives, shards(): lax.psum(select_rows(out_terms, group_members), 'mlp').astype(jnp.bfloat16)  74.3 us
    psum x1, blocking collectives, shards(): lax.psum(select_rows(low_terms, group_members).astype(jnp.bfloat16), 'mlp')  72.8 us
    all_gather x1, waiting for transfers between devices, shards(): whole = lax.all_gather(hidden_input, 'mlp', axis=1, tiled=True)  63.1 us
    all_gather x1, waiting for transfers between devices, shards(): kv_part = lax.all_gather(own_wkv, 'req', axis=0, tiled=True)  61.2 us
    all_gather x1, waiting for transfers between devices, shards(): lax.all_gather(output_weight, 'req', axis=2, tiled=True)  53.5 us
    all_gather x1, blocking collectives, shards(): lax.all_gather(request_key_value_up, 'req', axis=0, tiled=True)  36.1 us
    all_gather x1, blocking collectives, shards(): lax.all_gather(adapter_up_query, 'req', axis=0, tiled=True)  30.2 us
    all_gather x1, blocking collectives, shards(): lax.all_gather(adapter_up_output, 'req', axis=0, tiled=True)  30.1 us
  transfers between devices with their start and end apart: 6, of which 3 were waited for; matrix products, arithmetic and copies ran while one was open for 8% of the time, Pallas kernels for 0%

commit v1 on v0

--- a/solution.py
+++ b/solution.py
@@ -80,7 +80,20 @@
 ):
     feature_group_count = lax.axis_size("mlp")
     feature_group_index = lax.axis_index("mlp")
-    whole = lax.all_gather(hidden_input, "mlp", axis=1, tiled=True)
+    ways, here, step = (lax.axis_size("mlp"), lax.axis_index("mlp"), hidden_input.shape[1])
+    shape = [n * ways if d == 1 else n for d, n in enumerate(hidden_input.shape)]
+    whole = lax.dynamic_update_slice_in_dim(
+        jnp.zeros(shape, hidden_input.dtype), hidden_input, here * step, axis=1
+    )
+    going_up = going_down = hidden_input
+    for far in range(1, ways // 2 + 1):
+        going_up = lax.ppermute(going_up, "mlp", [(d, (d + 1) % ways) for d in range(ways)])
+        whole = lax.dynamic_update_slice_in_dim(whole, going_up, (here - far) % ways * step, axis=1)
+        if 2 * far < ways:
+            going_down = lax.ppermute(going_down, "mlp", [(d, (d - 1) % ways) for d in range(ways)])
+            whole = lax.dynamic_update_slice_in_dim(
+                whole, going_down, (here + far) % ways * step, axis=1
+            )
     row_count, full_width = whole.shape
     normalized_input = root_mean_scale(whole.astype(jnp.float32), input_norm_gain).astype(
         jnp.bfloat16

time: 520 us -> 450 us (0.87)
  waiting for transfers between devices: 180 us -> 32.3 us
  starting transfers between devices: 0.23 us -> 66.2 us
  local copies, waits for them, and re-layouts: 18.3 us -> 29.2 us
    ppermute x0 -> x15, starting transfers between devices: none -> 66 us  [the longest x7 49.2 us: shards(): lax.ppermute(going_down, 'mlp', [(d, (d - 1) % ways) for d in range(ways)])]
    all_gather x1 -> x0, waiting for transfers between devices: 63.1 us -> none  [shards(): whole = lax.all_gather(hidden_input, 'mlp', axis=1, tiled=True)]
    all_gather x1, waiting for transfers between devices: 61.2 us -> 0.01 us  [shards(): kv_part = lax.all_gather(own_wkv, 'req', axis=0, tiled=True)]
    all_gather x1, waiting for transfers between devices: 53.5 us -> 19.6 us  [shards(): lax.all_gather(output_weight, 'req', axis=2, tiled=True)]
    dynamic_update_slice x0 -> x16, local copies, waits for them, and re-layouts: none -> 11.5 us  [the longest x8 5.73 us: shards(): lax.dynamic_update_slice_in_dim(whole, going_up, (here - far) % ways * st...]
    ppermute x0 -> x15, waiting for transfers between devices: none -> 11.3 us  [the longest x8 11.2 us: shards(): lax.ppermute(going_up, 'mlp', [(d, (d + 1) % ways) for d in range(ways)])]
  transfers between devices with their start and end apart: 6 -> 20, of which waited for: 3 -> 8; matrix products, arithmetic and copies ran while one was open for 8% -> 13% of each run, Pallas kernels for 0% -> 0%
where the time goes in v1:
time: 450 us; the launch traced here: 449 us
  blocking collectives  270 us (60%)
  starting transfers between devices  66.2 us (15%)
  waiting for transfers between devices  32.3 us (7%)
  local copies, waits for them, and re-layouts  29.2 us (6%)
  matrix products  18.9 us (4%)
  other arithmetic  18.3 us (4%)
  between operations  14.6 us (3%)
    psum x1, blocking collectives, shards(): lax.psum(select_rows(out_terms, group_members), 'mlp').astype(jnp.bfloat16)  74.3 us
    psum x1, blocking collectives, shards(): lax.psum(select_rows(low_terms, group_members).astype(jnp.bfloat16), 'mlp')  69.8 us
    ppermute x7, starting transfers between devices, shards(): lax.ppermute(going_down, 'mlp', [(d, (d - 1) % ways) for d in range(ways)])  49.2 us
    all_gather x1, blocking collectives, shards(): lax.all_gather(request_key_value_up, 'req', axis=0, tiled=True)  35.8 us
    all_gather x1, blocking collectives, shards(): lax.all_gather(adapter_up_query, 'req', axis=0, tiled=True)  30.8 us
    all_gather x1, blocking collectives, shards(): lax.all_gather(adapter_up_output, 'req', axis=0, tiled=True)  30 us
    all_gather x1, blocking collectives, shards(): lax.all_gather(adapter_down_output, 'req', axis=0, tiled=True)  29.1 us
    all_gather x1, waiting for transfers between devices, shards(): lax.all_gather(output_weight, 'req', axis=2, tiled=True)  19.6 us
  transfers between devices with their start and end apart: 20, of which 8 were waited for; matrix products, arithmetic and copies ran while one was open for 13% of the time, Pallas kernels for 0%

profile of v1, /device:TPU:32, one launch (start us, length us, event | category | flops | bytes accessed | tf_op | source)
XLA Modules:
  0.0 449.2 jit_solution(9763253592710654498)
XLA Ops:
  9.7 3.4 collective-permute-start
  13.1 5.8 %collective-permute-start.1 = (bf16[384,256]{1,0:T(8,128)(2,1)}, bf16[384,256]{1,0:T(8,128)(2,1)S(1)}, u32[]{:S(2)}, u32[]{:S(2)}) collective-permute-start(bf16[384,256]{1,0:T(8,128)(2,1)} %param.20), channel_id=1, source_target_pairs={{0,15},{1,0},{2,1},{3,2},{4,3},{5,4},{6,5},{7,6},{8,7},{9,8},{10,9... | collective-permute-start | bytes 589832 | tf_op jit(solution)/shard_map/ppermute | solution.py:93
  25.6 35.8 %all_gather.26 = bf16[64,16,2,128]{3,1,2,0:T(8,128)(2,1)S(1)} all-gather(bf16[2,16,2,128]{3,1,2,0:T(8,128)(2,1)S(1)} %copy.66), channel_id=1, replica_groups=mesh['req'=32,'mlp'=16] {'req'}, dimensions={0}, use_global_device_ids=true | all-gather | bytes 540672 | tf_op jit(solution)/shard_map/all_gather | solution.py:119
  63.5 30.8 %all_gather.28 = bf16[64,16,256]{2,1,0:T(8,128)(2,1)S(1)} all-gather(bf16[2,16,256]{2,1,0:T(8,128)(2,1)} %param.29), channel_id=1, replica_groups=mesh['req'=32,'mlp'=16] {'req'}, dimensions={0}, use_global_device_ids=true | all-gather | bytes 540672 | tf_op jit(solution)/shard_map/all_gather | solution.py:118
  98.3 2.0 broadcast_in_dim.47
  103.9 1.9 collective-permute-start.2
  105.8 7.2 %collective-permute-start.3 = (bf16[384,256]{1,0:T(8,128)(2,1)S(1)}, bf16[384,256]{1,0:T(8,128)(2,1)S(1)}, u32[]{:S(2)}, u32[]{:S(2)}) collective-permute-start(bf16[384,256]{1,0:T(8,128)(2,1)S(1)} %collective-permute-done.1), channel_id=1, source_target_pairs={{0,15},{1,0},{2,1},{3,2},{4,3},{5,4},{6,5},{7,6},{8,7},{9,8},{10,9... | collective-permute-start | bytes 589832 | tf_op jit(solution)/shard_map/ppermute | solution.py:93
  116.3 1.9 collective-permute-start.4
  118.2 7.2 %collective-permute-start.5 = (bf16[384,256]{1,0:T(8,128)(2,1)S(1)}, bf16[384,256]{1,0:T(8,128)(2,1)S(1)}, u32[]{:S(2)}, u32[]{:S(2)}) collective-permute-start(bf16[384,256]{1,0:T(8,128)(2,1)S(1)} %collective-permute-done.3), channel_id=1, source_target_pairs={{0,15},{1,0},{2,1},{3,2},{4,3},{5,4},{6,5},{7,6},{8,7},{9,8},{10,9... | collective-permute-start | bytes 589832 | tf_op jit(solution)/shard_map/ppermute | solution.py:93
  127.8 1.9 collective-permute-start.6
  129.8 7.2 %collective-permute-start.7 = (bf16[384,256]{1,0:T(8,128)(2,1)S(1)}, bf16[384,256]{1,0:T(8,128)(2,1)S(1)}, u32[]{:S(2)}, u32[]{:S(2)}) collective-permute-start(bf16[384,256]{1,0:T(8,128)(2,1)S(1)} %collective-permute-done.5), channel_id=1, source_target_pairs={{0,15},{1,0},{2,1},{3,2},{4,3},{5,4},{6,5},{7,6},{8,7},{9,8},{10,9... | collective-permute-start | bytes 589832 | tf_op jit(solution)/shard_map/ppermute | solution.py:93
  138.7 1.9 collective-permute-start.8
  140.6 7.2 %collective-permute-start.9 = (bf16[384,256]{1,0:T(8,128)(2,1)S(1)}, bf16[384,256]{1,0:T(8,128)(2,1)S(1)}, u32[]{:S(2)}, u32[]{:S(2)}) collective-permute-start(bf16[384,256]{1,0:T(8,128)(2,1)S(1)} %collective-permute-done.7), channel_id=1, source_target_pairs={{0,15},{1,0},{2,1},{3,2},{4,3},{5,4},{6,5},{7,6},{8,7},{9,8},{10,9... | collective-permute-start | bytes 589832 | tf_op jit(solution)/shard_map/ppermute | solution.py:93
  149.6 1.9 collective-permute-start.10
  151.5 7.2 %collective-permute-start.11 = (bf16[384,256]{1,0:T(8,128)(2,1)S(1)}, bf16[384,256]{1,0:T(8,128)(2,1)S(1)}, u32[]{:S(2)}, u32[]{:S(2)}) collective-permute-start(bf16[384,256]{1,0:T(8,128)(2,1)S(1)} %collective-permute-done.9), channel_id=1, source_target_pairs={{0,15},{1,0},{2,1},{3,2},{4,3},{5,4},{6,5},{7,6},{8,7},{9,8},{10,9... | collective-permute-start | bytes 589832 | tf_op jit(solution)/shard_map/ppermute | solution.py:93
  160.4 1.9 collective-permute-start.12
  162.4 7.2 %collective-permute-start.13 = (bf16[384,256]{1,0:T(8,128)(2,1)S(1)}, bf16[384,256]{1,0:T(8,128)(2,1)S(1)}, u32[]{:S(2)}, u32[]{:S(2)}) collective-permute-start(bf16[384,256]{1,0:T(8,128)(2,1)S(1)} %collective-permute-done.11), channel_id=1, source_target_pairs={{0,15},{1,0},{2,1},{3,2},{4,3},{5,4},{6,5},{7,6},{8,7},{9,8},{10,9... | collective-permute-start | bytes 589832 | tf_op jit(solution)/shard_map/ppermute | solution.py:93
  171.3 1.9 collective-permute-start.14
  174.7 7.5 %collective-permute-done.14 = bf16[384,256]{1,0:T(8,128)(2,1)S(1)} collective-permute-done((bf16[384,256]{1,0:T(8,128)(2,1)S(1)}, bf16[384,256]{1,0:T(8,128)(2,1)S(1)}, u32[]{:S(2)}, u32[]{:S(2)}) %collective-permute-start.14) | collective-permute-done | bytes 196640 | tf_op jit(solution)/shard_map/ppermute | solution.py:90
  182.9 2.6 fusion
  185.5 4.6 %fusion.2 = bf16[384,4096]{1,0:T(8,128)(2,1)} fusion(bf16[384,4096]{1,0:T(8,128)(2,1)} %constant_dynamic-update-slice_fusion, f32[4096]{0:T(1024)S(1)} %convert_element_type.100, f32[384]{0:T(512)S(1)} %add_rsqrt_fusion.2), kind=kLoop, calls=%fused_computation.10 | loop fusion | flops 6291456 | bytes 6309376 | tf_op jit(solution)/shard_map/convert_element_type | solution.py:98
  190.1 2.0 gather_fusion.1
  193.3 69.8 %psum.14 = bf16[384,48]{0,1:T(8,128)(2,1)S(1)} all-reduce(bf16[384,48]{0,1:T(8,128)(2,1)S(1)} %fusion.25), channel_id=1, replica_groups=mesh['req'=32,'mlp'=16] {'mlp'}, use_global_device_ids=true, to_apply=%region_4.5 | all-reduce | flops 18432 | bytes 73728 | tf_op jit(solution)/shard_map/psum | solution.py:135
  265.2 4.7 %copy.61 = bf16[4096,2,128]{0,2,1:T(8,128)(2,1)S(1)} copy(bf16[4096,2,128]{2,1,0:T(2,128)(2,1)} %all-gather.5.cloned.1.call-done) | data formatting | bytes 4194304 | tf_op jit(solution)/shard_map/reshape | solution.py:141
  270.0 3.3 fusion.17
  274.1 3.9 multiply_reduce_fusion
  280.8 19.6 %all-gather.11.cloned.1.call-done = bf16[256,16,256]{0,2,1:T(8,128)(2,1)} async-done(((bf16[256,16,8]{0,2,1:T(8,128)(2,1)}), bf16[256,16,256]{0,2,1:T(8,128)(2,1)}) %all-gather.11.cloned.1.call-update) | async-done | bytes 2097168 | tf_op jit(solution)/shard_map/all_gather | solution.py:215
  300.4 4.3 convolution_convert_fusion
  305.4 29.1 %all_gather.30 = bf16[64,16,256]{2,1,0:T(8,128)(2,1)S(1)} all-gather(bf16[2,16,256]{2,1,0:T(8,128)(2,1)S(1)} %copy-done.4), channel_id=1, replica_groups=mesh['req'=32,'mlp'=16] {'req'}, dimensions={0}, use_global_device_ids=true | all-gather | bytes 540672 | tf_op jit(solution)/shard_map/all_gather | solution.py:117
  335.0 30.0 %all_gather.31 = bf16[64,16,256]{2,1,0:T(8,128)(2,1)S(1)} all-gather(bf16[2,16,256]{2,1,0:T(8,128)(2,1)S(1)} %copy-done.5), channel_id=1, replica_groups=mesh['req'=32,'mlp'=16] {'req'}, dimensions={0}, use_global_device_ids=true | all-gather | bytes 540672 | tf_op jit(solution)/shard_map/all_gather | solution.py:120
  365.8 74.3 %psum.15 = bf16[384,16]{0,1:T(8,128)(2,1)S(1)} all-reduce(f32[384,16]{0,1:T(8,128)S(1)} %fusion.26), channel_id=1, replica_groups=mesh['req'=32,'mlp'=16] {'mlp'}, use_global_device_ids=true, to_apply=%region_12.14 | all-reduce | flops 6144 | bytes 36864 | tf_op jit(solution)/shard_map/psum | solution.py:211
  440.8 1.9 fusion.16
  (130 shorter events, 42.5 us)
Async XLA Ops:
  7.2 1.0 copy-start
  7.2 90.0 %copy-start.13 = (s32[1,4]{1,0:T(1,128)S(1)}, s32[1,4]{1,0:T(1,128)}, u32[]{:S(2)}) copy-start(s32[1,4]{1,0:T(1,128)} %param.34) | copy-start | bytes 52
  7.2 90.1 %copy-start.10 = (s32[1,4,8]{2,1,0:T(4,128)S(1)}, s32[1,4,8]{2,1,0:T(4,128)}, u32[]{:S(2)}) copy-start(s32[1,4,8]{2,1,0:T(4,128)} %param.35) | copy-start | bytes 388
  7.2 182.9 %all-gather.7.cloned.1.call-start = ((), (), s32[]{:S(2)}) async-start(), calls=%async_computation.2 | async-start | bytes 1622016 | tf_op jit(solution)/shard_map/all_gather | solution.py:116
  7.9 257.3 %all-gather.5.cloned.1.call-start = ((), (), s32[]{:S(2)}) async-start(), calls=%async_computation.1 | async-start | bytes 2162688 | tf_op jit(solution)/shard_map/all_gather | solution.py:137
  8.9 265.2 %all-gather.9.cloned.1.call-start = ((), (), s32[]{:S(2)}) async-start(), calls=%async_computation.3 | async-start | bytes 2162688 | tf_op jit(solution)/shard_map/all_gather | solution.py:136
  9.7 290.8 %all-gather.11.cloned.1.call-start = ((), (), s32[]{:S(2)}) async-start(), calls=%async_computation.4 | async-start | bytes 2162688 | tf_op jit(solution)/shard_map/all_gather | solution.py:215
  9.7 94.2 %collective-permute-start = (bf16[384,256]{1,0:T(8,128)(2,1)}, bf16[384,256]{1,0:T(8,128)(2,1)S(1)}, u32[]{:S(2)}, u32[]{:S(2)}) collective-permute-start(bf16[384,256]{1,0:T(8,128)(2,1)} %param.20), channel_id=1, source_target_pairs={{0,1},{1,2},{2,3},{3,4},{4,5},{5,6},{6,7},{7,8},{8,9},{9,10},{10,1... | collective-permute-start | bytes 589832 | tf_op jit(solution)/shard_map/ppermute | solution.py:90
  13.1 92.7 %collective-permute-start.1 = (bf16[384,256]{1,0:T(8,128)(2,1)}, bf16[384,256]{1,0:T(8,128)(2,1)S(1)}, u32[]{:S(2)}, u32[]{:S(2)}) collective-permute-start(bf16[384,256]{1,0:T(8,128)(2,1)} %param.20), channel_id=1, source_target_pairs={{0,15},{1,0},{2,1},{3,2},{4,3},{5,4},{6,5},{7,6},{8,7},{9,8},{10,9... | collective-permute-start | bytes 589832 | tf_op jit(solution)/shard_map/ppermute | solution.py:93
  18.9 421.9 %reduce-scatter.2.cloned.1.call-start = ((), (), s32[]{:S(2)}) async-start(), calls=%async_computation.5 | async-start | bytes 3342336 | tf_op jit(solution)/shard_map/reduce_scatter | solution.py:218
  22.5 79.7 %copy-start.8 = (f32[64]{0:T(128)}, f32[64]{0:T(128)S(1)}, u32[]{:S(2)}) copy-start(f32[64]{0:T(128)S(1)} %multiply_exponential_fusion) | copy-start | bytes 772
  25.6 74.8 %copy-start.2 = (bf16[384,256]{1,0:T(8,128)(2,1)S(1)}, bf16[384,256]{1,0:T(8,128)(2,1)}, u32[]{:S(2)}) copy-start(bf16[384,256]{1,0:T(8,128)(2,1)} %param.20) | copy-start | bytes 589828
  103.9 88.2 %copy-start.6 = (f32[384,4]{0,1:T(4,128)}, f32[384,4]{0,1:T(4,128)S(1)}, u32[]{:S(2)}) copy-start(f32[384,4]{0,1:T(4,128)S(1)} %get-tuple-element.17) | copy-start | bytes 18436
  103.9 12.4 %collective-permute-start.2 = (bf16[384,256]{1,0:T(8,128)(2,1)S(1)}, bf16[384,256]{1,0:T(8,128)(2,1)S(1)}, u32[]{:S(2)}, u32[]{:S(2)}) collective-permute-start(bf16[384,256]{1,0:T(8,128)(2,1)S(1)} %collective-permute-done), channel_id=1, source_target_pairs={{0,1},{1,2},{2,3},{3,4},{4,5},{5,6},{6,7},{7,8},{8,9},{9,10},{10,1... | collective-permute-start | bytes 589832 | tf_op jit(solution)/shard_map/ppermute | solution.py:90
  105.8 12.3 %collective-permute-start.3 = (bf16[384,256]{1,0:T(8,128)(2,1)S(1)}, bf16[384,256]{1,0:T(8,128)(2,1)S(1)}, u32[]{:S(2)}, u32[]{:S(2)}) collective-permute-start(bf16[384,256]{1,0:T(8,128)(2,1)S(1)} %collective-permute-done.1), channel_id=1, source_target_pairs={{0,15},{1,0},{2,1},{3,2},{4,3},{5,4},{6,5},{7,6},{8,7},{9,8},{10,9... | collective-permute-start | bytes 589832 | tf_op jit(solution)/shard_map/ppermute | solution.py:93
  116.3 11.6 %collective-permute-start.4 = (bf16[384,256]{1,0:T(8,128)(2,1)S(1)}, bf16[384,256]{1,0:T(8,128)(2,1)S(1)}, u32[]{:S(2)}, u32[]{:S(2)}) collective-permute-start(bf16[384,256]{1,0:T(8,128)(2,1)S(1)} %collective-permute-done.2), channel_id=1, source_target_pairs={{0,1},{1,2},{2,3},{3,4},{4,5},{5,6},{6,7},{7,8},{8,9},{9,10},{10,1... | collective-permute-start | bytes 589832 | tf_op jit(solution)/shard_map/ppermute | solution.py:90
  118.2 11.5 %collective-permute-start.5 = (bf16[384,256]{1,0:T(8,128)(2,1)S(1)}, bf16[384,256]{1,0:T(8,128)(2,1)S(1)}, u32[]{:S(2)}, u32[]{:S(2)}) collective-permute-start(bf16[384,256]{1,0:T(8,128)(2,1)S(1)} %collective-permute-done.3), channel_id=1, source_target_pairs={{0,15},{1,0},{2,1},{3,2},{4,3},{5,4},{6,5},{7,6},{8,7},{9,8},{10,9... | collective-permute-start | bytes 589832 | tf_op jit(solution)/shard_map/ppermute | solution.py:93
  127.8 10.9 %collective-permute-start.6 = (bf16[384,256]{1,0:T(8,128)(2,1)S(1)}, bf16[384,256]{1,0:T(8,128)(2,1)S(1)}, u32[]{:S(2)}, u32[]{:S(2)}) collective-permute-start(bf16[384,256]{1,0:T(8,128)(2,1)S(1)} %collective-permute-done.4), channel_id=1, source_target_pairs={{0,1},{1,2},{2,3},{3,4},{4,5},{5,6},{6,7},{7,8},{8,9},{9,10},{10,1... | collective-permute-start | bytes 589832 | tf_op jit(solution)/shard_map/ppermute | solution.py:90
  129.8 10.9 %collective-permute-start.7 = (bf16[384,256]{1,0:T(8,128)(2,1)S(1)}, bf16[384,256]{1,0:T(8,128)(2,1)S(1)}, u32[]{:S(2)}, u32[]{:S(2)}) collective-permute-start(bf16[384,256]{1,0:T(8,128)(2,1)S(1)} %collective-permute-done.5), channel_id=1, source_target_pairs={{0,15},{1,0},{2,1},{3,2},{4,3},{5,4},{6,5},{7,6},{8,7},{9,8},{10,9... | collective-permute-start | bytes 589832 | tf_op jit(solution)/shard_map/ppermute | solution.py:93
  138.7 10.9 %collective-permute-start.8 = (bf16[384,256]{1,0:T(8,128)(2,1)S(1)}, bf16[384,256]{1,0:T(8,128)(2,1)S(1)}, u32[]{:S(2)}, u32[]{:S(2)}) collective-permute-start(bf16[384,256]{1,0:T(8,128)(2,1)S(1)} %collective-permute-done.6), channel_id=1, source_target_pairs={{0,1},{1,2},{2,3},{3,4},{4,5},{5,6},{6,7},{7,8},{8,9},{9,10},{10,1... | collective-permute-start | bytes 589832 | tf_op jit(solution)/shard_map/ppermute | solution.py:90
  140.6 10.9 %collective-permute-start.9 = (bf16[384,256]{1,0:T(8,128)(2,1)S(1)}, bf16[384,256]{1,0:T(8,128)(2,1)S(1)}, u32[]{:S(2)}, u32[]{:S(2)}) collective-permute-start(bf16[384,256]{1,0:T(8,128)(2,1)S(1)} %collective-permute-done.7), channel_id=1, source_target_pairs={{0,15},{1,0},{2,1},{3,2},{4,3},{5,4},{6,5},{7,6},{8,7},{9,8},{10,9... | collective-permute-start | bytes 589832 | tf_op jit(solution)/shard_map/ppermute | solution.py:93
  149.6 10.9 %collective-permute-start.10 = (bf16[384,256]{1,0:T(8,128)(2,1)S(1)}, bf16[384,256]{1,0:T(8,128)(2,1)S(1)}, u32[]{:S(2)}, u32[]{:S(2)}) collective-permute-start(bf16[384,256]{1,0:T(8,128)(2,1)S(1)} %collective-permute-done.8), channel_id=1, source_target_pairs={{0,1},{1,2},{2,3},{3,4},{4,5},{5,6},{6,7},{7,8},{8,9},{9,10},{10,1... | collective-permute-start | bytes 589832 | tf_op jit(solution)/shard_map/ppermute | solution.py:90
  151.5 10.9 %collective-permute-start.11 = (bf16[384,256]{1,0:T(8,128)(2,1)S(1)}, bf16[384,256]{1,0:T(8,128)(2,1)S(1)}, u32[]{:S(2)}, u32[]{:S(2)}) collective-permute-start(bf16[384,256]{1,0:T(8,128)(2,1)S(1)} %collective-permute-done.9), channel_id=1, source_target_pairs={{0,15},{1,0},{2,1},{3,2},{4,3},{5,4},{6,5},{7,6},{8,7},{9,8},{10,9... | collective-permute-start | bytes 589832 | tf_op jit(solution)/shard_map/ppermute | solution.py:93
  160.4 10.9 %collective-permute-start.12 = (bf16[384,256]{1,0:T(8,128)(2,1)S(1)}, bf16[384,256]{1,0:T(8,128)(2,1)S(1)}, u32[]{:S(2)}, u32[]{:S(2)}) collective-permute-start(bf16[384,256]{1,0:T(8,128)(2,1)S(1)} %collective-permute-done.10), channel_id=1, source_target_pairs={{0,1},{1,2},{2,3},{3,4},{4,5},{5,6},{6,7},{7,8},{8,9},{9,10},{10,1... | collective-permute-start | bytes 589832 | tf_op jit(solution)/shard_map/ppermute | solution.py:90
  162.4 11.6 %collective-permute-start.13 = (bf16[384,256]{1,0:T(8,128)(2,1)S(1)}, bf16[384,256]{1,0:T(8,128)(2,1)S(1)}, u32[]{:S(2)}, u32[]{:S(2)}) collective-permute-start(bf16[384,256]{1,0:T(8,128)(2,1)S(1)} %collective-permute-done.11), channel_id=1, source_target_pairs={{0,15},{1,0},{2,1},{3,2},{4,3},{5,4},{6,5},{7,6},{8,7},{9,8},{10,9... | collective-permute-start | bytes 589832 | tf_op jit(solution)/shard_map/ppermute | solution.py:93
  171.3 10.9 %collective-permute-start.14 = (bf16[384,256]{1,0:T(8,128)(2,1)S(1)}, bf16[384,256]{1,0:T(8,128)(2,1)S(1)}, u32[]{:S(2)}, u32[]{:S(2)}) collective-permute-start(bf16[384,256]{1,0:T(8,128)(2,1)S(1)} %collective-permute-done.12), channel_id=1, source_target_pairs={{0,1},{1,2},{2,3},{3,4},{4,5},{5,6},{6,7},{7,8},{8,9},{9,10},{10,1... | collective-permute-start | bytes 589832 | tf_op jit(solution)/shard_map/ppermute | solution.py:90
  270.0 3.4 copy-start.11
  270.0 3.5 copy-start.9
  274.1 4.2 copy-start.12
  278.5 1.4 copy-start.3
  304.7 30.3 %copy-start.5 = (bf16[2,16,256]{2,1,0:T(8,128)(2,1)S(1)}, bf16[2,16,256]{2,1,0:T(8,128)(2,1)}, u32[]{:S(2)}) copy-start(bf16[2,16,256]{2,1,0:T(8,128)(2,1)} %param.31) | copy-start | bytes 49156
  304.7 60.9 %copy-start.7 = (f32[384,4]{0,1:T(4,128)S(1)}, f32[384,4]{0,1:T(4,128)}, u32[]{:S(2)}) copy-start(f32[384,4]{0,1:T(4,128)} %copy-done.6) | copy-start | bytes 18436
  (2 other events, 1.7 us)
Sparse Core Ops, SparseCore 0:
  10.2 75.4 all-gather.6
  88.4 68.8 all-gather.4
  159.4 68.7 all-gather.8
  230.1 70.2 all-gather.10
  304.8 87.2 reduce-scatter.1
